TPU v7x, 128 devices: a whole 4x4x4 slice. The times are simulated.
128 devices in a mesh: owner: 4 (over y), worker: 32 (over x, z, core).
Axes of the slice: x: 4, y: 4, z: 4, core: 2. Of those that a mesh axis runs over, the one named last changes fastest.
Arguments:
- states: float32 [262144, 512], P(('owner', 'worker')), may hold values from -3 to 3
- row_of_user: int32 [262144], replicated, may hold values from 0 to 262143, as said below
- event_users: int32 [65536], P(('owner', 'worker')), may hold values from 0 to 262143, as said below
- event_features: int32 [65536], P(('owner', 'worker')), may hold values from 0 to 4095
- feature_table: bfloat16 [4096, 512], replicated, may hold values from -6 to 6
- gate_in: bfloat16 [512, 1536], replicated, may hold values from -0.25 to 0.25
- gate_state: bfloat16 [512, 1536], replicated, may hold values from -0.25 to 0.25
- tower_in: bfloat16 [4096, 1024], P(('owner', 'worker')), may hold values from -0.1875 to 0.1875
- tower_out: bfloat16 [512, 4096], P(('owner', 'worker')), may hold values from -0.09375 to 0.09375
Outputs:
- new_states: float32 [262144, 512], P(('owner', 'worker'))
- scores: float32 [65536], P(('owner', 'worker'))
Inputs may be any that keep to these rules, and one draw needn't show every extreme that they name: `row_of_user`: A permutation: each user has its own state row. `event_users`: among the 512 events of one device, at most 8 have their row (row_of_user of the user) in one device's block of 2048 rows, and for every device some block receives exactly 8 of its events.
All inputs are finite; a program needn't handle non-finite values.
Results may differ from a plain program's by a relative error of at most 0.0034.
Values may be sent and summed in bfloat16 or wider, within the bound.
A program may use at most 128 MiB of HBM per device.

v0:
```python
import jax
import jax.numpy as jnp
from jax import lax
from jax.sharding import PartitionSpec as P


def gru_cell(inputs, prior, gate_in, gate_state):
    gx = jnp.dot(inputs, gate_in, preferred_element_type=jnp.float32)
    gh = jnp.dot(prior, gate_state, preferred_element_type=jnp.float32)
    width = prior.shape[-1]
    reset = jax.nn.sigmoid(gx[:, :width] + gh[:, :width])
    update = jax.nn.sigmoid(gx[:, width : 2 * width] + gh[:, width : 2 * width])
    cand = jnp.tanh(gx[:, 2 * width :] + reset * gh[:, 2 * width :])
    return (1.0 - update) * cand + update * prior.astype(jnp.float32)


def per_device(
    states,
    row_of_user,
    event_users,
    event_features,
    feature_table,
    gate_in,
    gate_state,
    tower_in,
    tower_out,
):
    shards = lax.axis_size(("owner", "worker"))
    events = event_users.shape[0]
    row_count = states.shape[0]
    width = states.shape[1]
    cap = 2 * (events // shards)
    rows = row_of_user[event_users]
    target = rows // row_count
    local = rows - target * row_count
    inputs = feature_table[event_features]
    hits = (target[:, None] == jnp.arange(shards, dtype=jnp.int32)[None, :]).astype(jnp.int32)
    rank = jnp.sum((jnp.cumsum(hits, axis=0) - hits) * hits, axis=1)
    slot = target * cap + rank
    requests = jnp.full((shards * cap,), -1, jnp.int32).at[slot].set(local).reshape(shards, cap)
    asked = lax.all_to_all(requests, ("owner", "worker"), split_axis=0, concat_axis=0, tiled=True)
    fetched = states[jnp.maximum(asked, 0)].astype(jnp.bfloat16)
    arrived, asked = (
        lax.all_to_all(fetched, ("owner", "worker"), split_axis=0, concat_axis=0, tiled=True),
        asked,
    )
    prior = arrived.reshape(shards * cap, width)[slot]
    fresh = gru_cell(inputs, prior, gate_in, gate_state)
    fresh_low = fresh.astype(jnp.bfloat16)
    delta = fresh - prior.astype(jnp.float32)
    outgoing = (
        jnp.zeros((shards * cap, width), jnp.float32)
        .at[slot]
        .set(delta)
        .reshape(shards, cap, width)
    )
    changes = lax.all_to_all(outgoing, ("owner", "worker"), split_axis=0, concat_axis=0, tiled=True)
    valid = asked.reshape(-1) >= 0
    owners_ids = jnp.where(valid, asked.reshape(-1), row_count)
    total = jax.ops.segment_sum(changes.reshape(-1, width), owners_ids, num_segments=row_count + 1)[
        :row_count
    ]
    count = jax.ops.segment_sum(valid.astype(jnp.int32), owners_ids, num_segments=row_count + 1)[
        :row_count
    ]
    new_states = states + total / jnp.maximum(count, 1).astype(jnp.float32)[:, None]
    joined = jnp.concatenate([fresh_low, inputs], axis=1)
    hidden = jax.nn.gelu(
        lax.dot_general(
            joined,
            lax.all_gather(tower_in, ("owner", "worker"), axis=0, tiled=True),
            (((1,), (1,)), ((), ())),
            preferred_element_type=jnp.float32,
        )
    ).astype(jnp.bfloat16)
    tower = lax.dot_general(
        hidden,
        lax.all_gather(tower_out, ("owner", "worker"), axis=0, tiled=True),
        (((1,), (1,)), ((), ())),
        preferred_element_type=jnp.float32,
    )
    scores = jnp.sum(tower * inputs.astype(jnp.float32), axis=1) / jnp.sqrt(jnp.float32(width))
    return (new_states, scores)


def solution(mesh):
    placed = (
        P(("owner", "worker"), None),
        P(),
        P(("owner", "worker")),
        P(("owner", "worker")),
        P(),
        P(),
        P(),
        P(("owner", "worker"), None),
        P(("owner", "worker"), None),
    )
    return jax.shard_map(
        per_device,
        mesh=mesh,
        in_specs=placed,
        out_specs=(P(("owner", "worker"), None), P(("owner", "worker"))),
        check_vma=False,
    )
```

profile of v0, /device:TPU:1, one launch (start us, length us, event | category | flops | bytes accessed | tf_op | source)
XLA Modules:
  0.0 186.0 jit_solution(2126969948334331115)
XLA Ops:
  7.2 0.7 all-gather.6.cloned.1.call-update
  8.0 0.7 all-gather.4.cloned.1.call-update
  8.7 0.7 compare_select_fusion.3
  9.4 6.5 %gather_fusion = s32[512]{0:T(512)S(1)} fusion(s32[262144]{0:T(1024)} %param.10, s32[1024]{0:T(1024)S(1)} %pad_clamp_fusion.2), kind=kCustom, calls=%fused_computation | custom fusion | bytes 6144 | tf_op jit(solution)/shard_map/gather | solution.py:33
  16.6 2.4 %scatter_custom_fusion = s32[1024]{0:T(1024)S(1)} fusion(s32[512]{0:T(512)S(1)} %bitcast.59, s32[512]{0:T(512)S(1)} %get-tuple-element.7, s32[]{:T(128)} %constant.17.clone.1), kind=kCustom, calls=%fused_computation.93 | custom fusion | bytes 4100 | tf_op jit(solution)/shard_map/scatter | solution.py:40
  19.1 20.7 %all_to_all.19 = s32[128,1,8]{2,1,0:T(1,128)S(1)} all-to-all(s32[128,1,8]{2,1,0:T(1,128)S(1)} %bitcast.54), channel_id=1, replica_groups=mesh['owner'=4,'worker'=32] {'owner','worker'}, dimensions={0} | all-to-all | bytes 8192 | tf_op jit(solution)/shard_map/all_to_all | solution.py:41
  40.4 1.2 fusion.49
  41.7 7.3 %gather_fusion.2 = bf16[1024,512]{1,0:T(8,128)(2,1)} fusion(f32[2048,512]{1,0:T(8,128)} %param.9, s32[1024]{0:T(1024)S(1)} %broadcast_clamp_fusion), kind=kCustom, calls=%fused_computation.2 | custom fusion | bytes 2101248 | tf_op jit(solution)/shard_map/gather | solution.py:42
  49.0 4.6 %all-to-all-start.1 = ((bf16[128,8,512]{2,1,0:T(8,128)(2,1)}), bf16[128,8,512]{2,1,0:T(8,128)(2,1)S(1)}, u32[]{:S(2)}, u32[]{:S(2)}) async-start(bf16[128,8,512]{2,1,0:T(8,128)(2,1)} %bitcast.51), calls=%async_computation.1 | async-start | bytes 2097152 | tf_op jit(solution)/shard_map/all_to_all | solution.py:44
  53.6 4.7 %gather_fusion.1 = bf16[512,512]{1,0:T(8,128)(2,1)S(1)} fusion(bf16[4096,512]{1,0:T(8,128)(2,1)} %param.13, s32[1024]{0:T(1024)S(1)} %pad_clamp_fusion.1), kind=kCustom, calls=%fused_computation.1 | custom fusion | bytes 1050624 | tf_op jit(solution)/shard_map/gather | solution.py:36
  58.4 2.6 %fusion.68 = f32[512,1536]{1,0:T(8,128)} fusion(bf16[512,512]{1,0:T(8,128)(2,1)S(1)} %gather_fusion.1, bf16[512,1536]{1,0:T(8,128)(2,1)S(1)} %copy-done), kind=kOutput, calls=%fused_computation.104 | convolution fusion | flops 805306368 | bytes 5242880 | tf_op jit(solution)/shard_map/dot_general | solution.py:8
  61.0 11.9 %all-to-all-done.1 = bf16[128,8,512]{2,1,0:T(8,128)(2,1)S(1)} async-done(((bf16[128,8,512]{2,1,0:T(8,128)(2,1)}), bf16[128,8,512]{2,1,0:T(8,128)(2,1)S(1)}, u32[]{:S(2)}, u32[]{:S(2)}) %all-to-all-start.1) | async-done | bytes 1048608 | tf_op jit(solution)/shard_map/all_to_all | solution.py:44
  72.9 2.0 %gather_fusion.3 = bf16[512,512]{1,0:T(8,128)(2,1)S(1)} fusion(bf16[1024,512]{1,0:T(8,128)(2,1)S(1)} %bitcast.49, s32[1024]{0:T(1024)S(1)} %pad_clamp_fusion), kind=kCustom, calls=%fused_computation.3 | custom fusion | bytes 1050624 | tf_op jit(solution)/shard_map/gather | solution.py:47
  74.9 2.6 %fusion.69 = f32[512,1536]{1,0:T(8,128)S(1)} fusion(bf16[512,512]{1,0:T(8,128)(2,1)S(1)} %gather_fusion.3, bf16[512,1536]{1,0:T(8,128)(2,1)} %param.15), kind=kOutput, calls=%fused_computation.105 | convolution fusion | flops 805306368 | bytes 5242880 | tf_op jit(solution)/shard_map/dot_general | solution.py:9
  77.5 1.9 %fusion.66 = (bf16[512,512]{1,0:T(8,128)(2,1)S(1)}, f32[512,512]{1,0:T(8,128)}) fusion(bf16[512,512]{1,0:T(8,128)(2,1)S(1)} %gather_fusion.3, f32[512,1536]{1,0:T(8,128)S(1)} %fusion.69, f32[512,1536]{1,0:T(8,128)S(1)} %copy-done.1), kind=kLoop, calls=%fused_computation.103 | loop fusion | flops 4194304 | bytes 8388608 | tf_op jit(solution)/shard_map/convert_element_type | solution.py:49
  79.4 4.4 %scatter_custom_fusion.1 = f32[1024,512]{1,0:T(8,128)} fusion(s32[512]{0:T(512)S(1)} %bitcast.61, f32[512,512]{1,0:T(8,128)} %get-tuple-element.6, bf16[512,512]{1,0:T(8,128)(2,1)S(1)} %gather_fusion.3, f32[]{:T(128)} %constant.16.clone.1), kind=kCustom, calls=%fused_computation.28 | custom fusion | flops 524288 | bytes 3670020 | tf_op jit(solution)/shard_map/scatter | solution.py:54
  83.8 5.7 %all-to-all-start.2 = ((f32[128,8,512]{2,1,0:T(8,128)}), f32[128,8,512]{2,1,0:T(8,128)}, u32[]{:S(2)}, u32[]{:S(2)}) async-start(f32[128,8,512]{2,1,0:T(8,128)} %bitcast.50), calls=%async_computation.2 | async-start | bytes 4194304 | tf_op jit(solution)/shard_map/all_to_all | solution.py:57
  89.9 6.8 %scatter_custom_fusion.3 = s32[2049]{0:T(1024)S(1)} fusion(s32[1024]{0:T(1024)S(1)} %bitcast.62, s32[1024]{0:T(1024)S(1)} %reshape.212, s32[]{:T(128)} %constant.18.clone.1), kind=kCustom, calls=%fused_computation.66 | custom fusion | flops 1024 | bytes 8200 | tf_op jit(solution)/shard_map/scatter-add | solution.py:63
  96.7 23.3 %all-to-all-done.2 = f32[128,8,512]{2,1,0:T(8,128)} async-done(((f32[128,8,512]{2,1,0:T(8,128)}), f32[128,8,512]{2,1,0:T(8,128)}, u32[]{:S(2)}, u32[]{:S(2)}) %all-to-all-start.2) | async-done | bytes 2097184 | tf_op jit(solution)/shard_map/all_to_all | solution.py:57
  120.0 9.8 %scatter_custom_fusion.2 = f32[2049,512]{1,0:T(8,128)} fusion(s32[1024]{0:T(1024)S(1)} %bitcast.63, f32[]{:T(128)} %constant.16.clone.1, f32[128,8,512]{2,1,0:T(8,128)} %all-to-all-done.2), kind=kCustom, calls=%fused_computation.20 | custom fusion | flops 524288 | bytes 6293508 | tf_op jit(solution)/shard_map/scatter-add | solution.py:60
  129.8 6.1 %fusion.8 = f32[2048,512]{1,0:T(8,128)} fusion(f32[2048,512]{1,0:T(8,128)} %param.9, f32[2049,512]{1,0:T(8,128)} %scatter_custom_fusion.2, f32[2048]{0:T(1024)S(1)} %fusion.50), kind=kLoop, calls=%fused_computation.18 | loop fusion | flops 2097152 | bytes 12591104 | tf_op jit(solution)/shard_map/add | solution.py:66
  135.9 6.9 %reshape.222 = bf16[512,4096]{1,0:T(8,128)(2,1)} reshape(bf16[128,4,4096]{2,1,0:T(4,128)(2,1)} %all-gather.6.cloned.1.call-done) | data formatting | bytes 8388608
  142.8 24.3 %all-gather.4.cloned.1.call-done = bf16[4096,1024]{1,0:T(8,128)(2,1)} async-done(((bf16[32,1024]{1,0:T(8,128)(2,1)}), bf16[4096,1024]{1,0:T(8,128)(2,1)}) %all-gather.4.cloned.1.call-update) | async-done | bytes 8388624 | tf_op jit(solution)/shard_map/all_gather | solution.py:71
  167.1 11.4 %fusion.17 = f32[512]{0:T(512)S(1)} fusion(bf16[512,4096]{1,0:T(8,128)(2,1)} %reshape.222, bf16[4096,1024]{1,0:T(8,128)(2,1)} %all-gather.4.cloned.1.call-done, bf16[512,512]{1,0:T(8,128)(2,1)S(1)} %copy-done.3, bf16[512,512]{1,0:T(8,128)(2,1)S(1)} %get-tuple-element.5, bf16[512,512]{0,1:T(8,128)(2,1)S(1)} %copy.18), kind=kOutput, calls=%fused_computation.26 | convolution fusion | flops 6464208384 | bytes 14157824 | tf_op jit(solution)/shard_map/dot_general | solution.py:76
  (39 shorter events, 2.5 us)
Async XLA Ops:
  7.2 51.2 %copy-start = (bf16[512,1536]{1,0:T(8,128)(2,1)S(1)}, bf16[512,1536]{1,0:T(8,128)(2,1)}, u32[]{:S(2)}) copy-start(bf16[512,1536]{1,0:T(8,128)(2,1)} %param.14) | copy-start | bytes 4718596
  7.2 128.7 %all-gather.6.cloned.1.call-start = ((), (), s32[]{:S(2)}) async-start(), calls=%async_computation.4 | async-start | bytes 4227072 | tf_op jit(solution)/shard_map/all_gather | solution.py:78
  7.9 159.2 %all-gather.4.cloned.1.call-start = ((), (), s32[]{:S(2)}) async-start(), calls=%async_computation.3 | async-start | bytes 8454144 | tf_op jit(solution)/shard_map/all_gather | solution.py:71
  41.6 11.9 %copy-start.4 = (s32[512]{0:T(512)S(1)}, s32[512]{0:T(512)}, u32[]{:S(2)}) copy-start(s32[512]{0:T(512)} %param.12) | copy-start | bytes 6148
  49.0 24.0 %all-to-all-start.1 = ((bf16[128,8,512]{2,1,0:T(8,128)(2,1)}), bf16[128,8,512]{2,1,0:T(8,128)(2,1)S(1)}, u32[]{:S(2)}, u32[]{:S(2)}) async-start(bf16[128,8,512]{2,1,0:T(8,128)(2,1)} %bitcast.51), calls=%async_computation.1 | async-start | bytes 2097152 | tf_op jit(solution)/shard_map/all_to_all | solution.py:44
  58.3 14.6 %copy-start.2 = (bf16[512,512]{1,0:T(8,128)(2,1)}, bf16[512,512]{1,0:T(8,128)(2,1)S(1)}, u32[]{:S(2)}) copy-start(bf16[512,512]{1,0:T(8,128)(2,1)S(1)} %gather_fusion.1) | copy-start | bytes 1572868
  74.9 2.6 %copy-start.1 = (f32[512,1536]{1,0:T(8,128)S(1)}, f32[512,1536]{1,0:T(8,128)}, u32[]{:S(2)}) copy-start(f32[512,1536]{1,0:T(8,128)} %fusion.68) | copy-start | bytes 9437188
  79.4 10.1 %copy-start.3 = (bf16[512,512]{1,0:T(8,128)(2,1)S(1)}, bf16[512,512]{1,0:T(8,128)(2,1)}, u32[]{:S(2)}) copy-start(bf16[512,512]{1,0:T(8,128)(2,1)} %copy-done.2) | copy-start | bytes 1572868
  83.8 36.2 %all-to-all-start.2 = ((f32[128,8,512]{2,1,0:T(8,128)}), f32[128,8,512]{2,1,0:T(8,128)}, u32[]{:S(2)}, u32[]{:S(2)}) async-start(f32[128,8,512]{2,1,0:T(8,128)} %bitcast.50), calls=%async_computation.2 | async-start | bytes 4194304 | tf_op jit(solution)/shard_map/all_to_all | solution.py:57
Sparse Core Ops, SparseCore 0:
  11.2 73.3 all-gather.5
  87.6 79.5 all-gather.3
where the time goes:
time: 187 us; the launch traced here: 186 us
  waiting for transfers between devices  60.9 us (33%)
  other arithmetic  32 us (17%)
  local copies, waits for them, and re-layouts  31.1 us (17%)
  blocking collectives  20.7 us (11%)
  matrix products  16.6 us (9%)
  between operations  14.3 us (8%)
  starting transfers between devices  10.3 us (6%)
    all_gather x1, waiting for transfers between devices, per_device(): lax.all_gather(tower_in, ('owner', 'worker'), axis=0, tiled=True)  24.3 us
    all_to_all x1, waiting for transfers between devices, per_device(): lax.all_to_all(outgoing, ('owner', 'worker'), split_axis=0, concat_axis=0...  23.3 us
    all_to_all x1, blocking collectives, per_device(): lax.all_to_all(requests, ('owner', 'worker'), split_axis=0, concat_axis=0...  20.7 us
    all_to_all x1, waiting for transfers between devices, per_device(): lax.all_to_all(fetched, ('owner', 'worker'), split_axis=0, concat_axis=0,...  11.9 us
    dot_general x1, matrix products, per_device(): lax.dot_general(hidden, lax.all_gather(tower_out, ('owner', 'worker'), ax...  11.4 us
    scatter-add x1, other arithmetic, per_device(): jax.ops.segment_sum(changes.reshape(-1, width), owners_ids, num_segments=...  9.8 us
    gather x1, local copies, waits for them, and re-layouts, per_device(): fetched = states[jnp.maximum(asked, 0)].astype(jnp.bfloat16)  7.29 us
    unnamed x12, local copies, waits for them, and re-layouts  6.97 us
  transfers between devices with their start and end apart: 4, of which 3 were waited for; matrix products, arithmetic and copies ran while one was open for 36% of the time, Pallas kernels for 0%

commit v1 on v0

--- a/solution.py
+++ b/solution.py
@@ -68,7 +68,15 @@
     hidden = jax.nn.gelu(
         lax.dot_general(
             joined,
-            lax.all_gather(tower_in, ("owner", "worker"), axis=0, tiled=True),
+            jnp.concatenate(
+                lax.all_to_all(
+                    jnp.stack([tower_in] * lax.axis_size(("owner", "worker"))),
+                    ("owner", "worker"),
+                    0,
+                    0,
+                ),
+                axis=0,
+            ),
             (((1,), (1,)), ((), ())),
             preferred_element_type=jnp.float32,
         )

time: 187 us -> 274 us (1.47)
  waiting for transfers between devices: 60.9 us -> 139 us
  starting transfers between devices: 10.3 us -> 16.6 us
  local copies, waits for them, and re-layouts: 31.1 us -> 35.4 us
    all_gather x1, waiting for transfers between devices: 0.01 us -> 97.1 us  [per_device(): lax.all_gather(tower_out, ('owner', 'worker'), axis=0, tiled=True)]
    all_gather x1 -> x0, waiting for transfers between devices: 24.3 us -> none  [per_device(): lax.all_gather(tower_in, ('owner', 'worker'), axis=0, tiled=True)]
    all_to_all x1, waiting for transfers between devices: 23.3 us -> 29.4 us  [per_device(): lax.all_to_all(outgoing, ('owner', 'worker'), split_axis=0, concat_axis=0...]
    all_to_all x0 -> x1, starting transfers between devices: none -> 6.04 us  [per_device(): lax.all_to_all(jnp.stack([tower_in] * lax.axis_size(('owner', 'worker')))...]
    another operation x3 -> x4, local copies, waits for them, and re-layouts: 0.03 us -> 4.31 us  [the longest x1 4.28 us: per_device(): jnp.stack([tower_in] * lax.axis_size(('owner', 'worker')))]
    unnamed x12 -> x16, local copies, waits for them, and re-layouts: 6.97 us -> 6.96 us
  transfers between devices with their start and end apart: 4 -> 4, of which waited for: 3 -> 3; matrix products, arithmetic and copies ran while one was open for 36% -> 15% of each run, Pallas kernels for 0% -> 0%
where the time goes in v1:
time: 274 us; the launch traced here: 273 us
  waiting for transfers between devices  139 us (51%)
  local copies, waits for them, and re-layouts  35.4 us (13%)
  other arithmetic  31 us (11%)
  blocking collectives  20.7 us (8%)
  starting transfers between devices  16.6 us (6%)
  matrix products  16.6 us (6%)
  between operations  14.3 us (5%)
    all_gather x1, waiting for transfers between devices, per_device(): lax.all_gather(tower_out, ('owner', 'worker'), axis=0, tiled=True)  97.1 us
    all_to_all x1, waiting for transfers between devices, per_device(): lax.all_to_all(outgoing, ('owner', 'worker'), split_axis=0, concat_axis=0...  29.4 us
    all_to_all x1, blocking collectives, per_device(): lax.all_to_all(requests, ('owner', 'worker'), split_axis=0, concat_axis=0...  20.7 us
    all_to_all x1, waiting for transfers between devices, per_device(): lax.all_to_all(fetched, ('owner', 'worker'), split_axis=0, concat_axis=0,...  11.9 us
    dot_general x1, matrix products, per_device(): lax.dot_general(hidden, lax.all_gather(tower_out, ('owner', 'worker'), ax...  11.4 us
    scatter-add x1, other arithmetic, per_device(): jax.ops.segment_sum(changes.reshape(-1, width), owners_ids, num_segments=...  9.77 us
    gather x1, local copies, waits for them, and re-layouts, per_device(): fetched = states[jnp.maximum(asked, 0)].astype(jnp.bfloat16)  7.3 us
    unnamed x16, local copies, waits for them, and re-layouts  6.96 us
  transfers between devices with their start and end apart: 4, of which 3 were waited for; matrix products, arithmetic and copies ran while one was open for 15% of the time, Pallas kernels for 0%

profile of v1, /device:TPU:1, one launch (start us, length us, event | category | flops | bytes accessed | tf_op | source)
XLA Modules:
  0.0 273.5 jit_solution(6361044122485502325)
XLA Ops:
  7.2 0.8 compare_select_fusion.3
  8.0 6.5 %gather_fusion = s32[512]{0:T(512)S(1)} fusion(s32[262144]{0:T(1024)} %param.10, s32[1024]{0:T(1024)S(1)} %pad_clamp_fusion.2), kind=kCustom, calls=%fused_computation | custom fusion | bytes 6144 | tf_op jit(solution)/shard_map/gather | solution.py:33
  15.2 2.4 scatter_custom_fusion
  17.8 20.7 %all_to_all.24 = s32[128,1,8]{2,1,0:T(1,128)S(1)} all-to-all(s32[128,1,8]{2,1,0:T(1,128)S(1)} %bitcast.55), channel_id=1, replica_groups=mesh['owner'=4,'worker'=32] {'owner','worker'}, dimensions={0} | all-to-all | bytes 8192 | tf_op jit(solution)/shard_map/all_to_all | solution.py:41
  39.0 1.2 fusion.49
  40.3 7.3 %gather_fusion.2 = bf16[1024,512]{1,0:T(8,128)(2,1)} fusion(f32[2048,512]{1,0:T(8,128)} %param.9, s32[1024]{0:T(1024)S(1)} %broadcast_clamp_fusion), kind=kCustom, calls=%fused_computation.2 | custom fusion | bytes 2101248 | tf_op jit(solution)/shard_map/gather | solution.py:42
  47.6 4.6 %all-to-all-start.1 = ((bf16[128,8,512]{2,1,0:T(8,128)(2,1)}), bf16[128,8,512]{2,1,0:T(8,128)(2,1)S(1)}, u32[]{:S(2)}, u32[]{:S(2)}) async-start(bf16[128,8,512]{2,1,0:T(8,128)(2,1)} %bitcast.52), calls=%async_computation.1 | async-start | bytes 2097152 | tf_op jit(solution)/shard_map/all_to_all | solution.py:44
  52.2 4.7 %gather_fusion.1 = bf16[512,512]{1,0:T(8,128)(2,1)S(1)} fusion(bf16[4096,512]{1,0:T(8,128)(2,1)} %param.13, s32[1024]{0:T(1024)S(1)} %pad_clamp_fusion.1), kind=kCustom, calls=%fused_computation.1 | custom fusion | bytes 1050624 | tf_op jit(solution)/shard_map/gather | solution.py:36
  57.0 2.6 fusion.68
  59.6 11.9 %all-to-all-done.1 = bf16[128,8,512]{2,1,0:T(8,128)(2,1)S(1)} async-done(((bf16[128,8,512]{2,1,0:T(8,128)(2,1)}), bf16[128,8,512]{2,1,0:T(8,128)(2,1)S(1)}, u32[]{:S(2)}, u32[]{:S(2)}) %all-to-all-start.1) | async-done | bytes 1048608 | tf_op jit(solution)/shard_map/all_to_all | solution.py:44
  71.5 2.0 gather_fusion.3
  73.5 2.5 fusion.69
  76.0 1.7 fusion.66
  77.7 3.7 %scatter_custom_fusion.1 = f32[1024,512]{1,0:T(8,128)} fusion(s32[512]{0:T(512)S(1)} %bitcast.62, f32[512,512]{1,0:T(8,128)S(1)} %get-tuple-element.6, bf16[512,512]{1,0:T(8,128)(2,1)S(1)} %gather_fusion.3, f32[]{:T(128)} %constant.16.clone.1), kind=kCustom, calls=%fused_computation.28 | custom fusion | flops 524288 | bytes 3670020 | tf_op jit(solution)/shard_map/scatter | solution.py:54
  81.4 5.7 %all-to-all-start.2 = ((f32[128,8,512]{2,1,0:T(8,128)}), f32[128,8,512]{2,1,0:T(8,128)}, u32[]{:S(2)}, u32[]{:S(2)}) async-start(f32[128,8,512]{2,1,0:T(8,128)} %bitcast.51), calls=%async_computation.2 | async-start | bytes 4194304 | tf_op jit(solution)/shard_map/all_to_all | solution.py:57
  87.9 29.4 %all-to-all-done.2 = f32[128,8,512]{2,1,0:T(8,128)} async-done(((f32[128,8,512]{2,1,0:T(8,128)}), f32[128,8,512]{2,1,0:T(8,128)}, u32[]{:S(2)}, u32[]{:S(2)}) %all-to-all-start.2) | async-done | bytes 2097184 | tf_op jit(solution)/shard_map/all_to_all | solution.py:57
  117.3 4.3 %stack.2 = bf16[128,32,1024]{2,1,0:T(8,128)(2,1)} broadcast(bf16[32,1024]{1,0:T(8,128)(2,1)S(1)} %copy-done.5), dimensions={1,2} | broadcast | bytes 8454144 | tf_op jit(solution)/shard_map/stack | solution.py:73
  121.6 6.0 %all-to-all-start.3 = ((bf16[128,32,1024]{2,1,0:T(8,128)(2,1)}), bf16[128,32,1024]{2,1,0:T(8,128)(2,1)}, u32[]{:S(2)}, u32[]{:S(2)}) async-start(bf16[128,32,1024]{2,1,0:T(8,128)(2,1)} %stack.2), calls=%async_computation.3 | async-start | bytes 16777216 | tf_op jit(solution)/shard_map/all_to_all | solution.py:72
  128.1 6.8 %scatter_custom_fusion.3 = s32[2049]{0:T(1024)S(1)} fusion(s32[1024]{0:T(1024)S(1)} %bitcast.63, s32[1024]{0:T(1024)S(1)} %reshape.218, s32[]{:T(128)} %constant.18.clone.1), kind=kCustom, calls=%fused_computation.66 | custom fusion | flops 1024 | bytes 8200 | tf_op jit(solution)/shard_map/scatter-add | solution.py:63
  134.9 9.8 %scatter_custom_fusion.2 = f32[2049,512]{1,0:T(8,128)} fusion(s32[1024]{0:T(1024)S(1)} %bitcast.64, f32[]{:T(128)} %constant.16.clone.1, f32[128,8,512]{2,1,0:T(8,128)} %all-to-all-done.2), kind=kCustom, calls=%fused_computation.20 | custom fusion | flops 524288 | bytes 6293508 | tf_op jit(solution)/shard_map/scatter-add | solution.py:60
  144.6 6.0 %fusion.8 = f32[2048,512]{1,0:T(8,128)} fusion(f32[2048,512]{1,0:T(8,128)} %param.9, f32[2049,512]{1,0:T(8,128)} %scatter_custom_fusion.2, f32[2048]{0:T(1024)S(1)} %fusion.50), kind=kLoop, calls=%fused_computation.18 | loop fusion | flops 2097152 | bytes 12591104 | tf_op jit(solution)/shard_map/add | solution.py:66
  150.6 97.1 %all-gather.3.cloned.1.call-done = bf16[128,4,4096]{2,1,0:T(4,128)(2,1)} async-done(((bf16[1,4,4096]{2,1,0:T(4,128)(2,1)}), bf16[128,4,4096]{2,1,0:T(4,128)(2,1)}) %all-gather.3.cloned.1.call-update) | async-done | bytes 4194320 | tf_op jit(solution)/shard_map/all_gather | solution.py:86
  247.7 6.9 %reshape.228 = bf16[512,4096]{1,0:T(8,128)(2,1)} reshape(bf16[128,4,4096]{2,1,0:T(4,128)(2,1)} %all-gather.3.cloned.1.call-done) | data formatting | bytes 8388608
  254.6 11.4 %fusion.17 = f32[512]{0:T(512)S(1)} fusion(bf16[512,4096]{1,0:T(8,128)(2,1)} %reshape.228, bf16[4096,1024]{1,0:T(8,128)(2,1)} %bitcast.13, bf16[512,512]{1,0:T(8,128)(2,1)S(1)} %copy-done.3, bf16[512,512]{1,0:T(8,128)(2,1)S(1)} %copy-done.4, bf16[512,512]{0,1:T(8,128)(2,1)S(1)} %copy.18), kind=kOutput, calls=%fused_computation.26 | convolution fusion | flops 6464208384 | bytes 14157824 | tf_op jit(solution)/shard_map/dot_general | solution.py:84
  (43 shorter events, 3.1 us)
Async XLA Ops:
  7.2 49.8 %copy-start = (bf16[512,1536]{1,0:T(8,128)(2,1)S(1)}, bf16[512,1536]{1,0:T(8,128)(2,1)}, u32[]{:S(2)}) copy-start(bf16[512,1536]{1,0:T(8,128)(2,1)} %param.14) | copy-start | bytes 4718596
  40.3 11.9 %copy-start.6 = (s32[512]{0:T(512)S(1)}, s32[512]{0:T(512)}, u32[]{:S(2)}) copy-start(s32[512]{0:T(512)} %param.12) | copy-start | bytes 6148
  47.6 23.9 %all-to-all-start.1 = ((bf16[128,8,512]{2,1,0:T(8,128)(2,1)}), bf16[128,8,512]{2,1,0:T(8,128)(2,1)S(1)}, u32[]{:S(2)}, u32[]{:S(2)}) async-start(bf16[128,8,512]{2,1,0:T(8,128)(2,1)} %bitcast.52), calls=%async_computation.1 | async-start | bytes 2097152 | tf_op jit(solution)/shard_map/all_to_all | solution.py:44
  57.0 14.5 %copy-start.2 = (bf16[512,512]{1,0:T(8,128)(2,1)}, bf16[512,512]{1,0:T(8,128)(2,1)S(1)}, u32[]{:S(2)}) copy-start(bf16[512,512]{1,0:T(8,128)(2,1)S(1)} %gather_fusion.1) | copy-start | bytes 1572868
  73.5 2.6 copy-start.1
  77.7 39.6 %copy-start.5 = (bf16[32,1024]{1,0:T(8,128)(2,1)S(1)}, bf16[32,1024]{1,0:T(8,128)(2,1)}, u32[]{:S(2)}) copy-start(bf16[32,1024]{1,0:T(8,128)(2,1)} %param.16) | copy-start | bytes 196612
  81.4 35.9 %all-to-all-start.2 = ((f32[128,8,512]{2,1,0:T(8,128)}), f32[128,8,512]{2,1,0:T(8,128)}, u32[]{:S(2)}, u32[]{:S(2)}) async-start(f32[128,8,512]{2,1,0:T(8,128)} %bitcast.51), calls=%async_computation.2 | async-start | bytes 4194304 | tf_op jit(solution)/shard_map/all_to_all | solution.py:57
  87.1 160.5 %all-gather.3.cloned.1.call-start = ((), (), s32[]{:S(2)}) async-start(), calls=%async_computation.4 | async-start | bytes 4227072 | tf_op jit(solution)/shard_map/all_gather | solution.py:86
  121.6 6.1 %copy-start.3 = (bf16[512,512]{1,0:T(8,128)(2,1)S(1)}, bf16[512,512]{1,0:T(8,128)(2,1)}, u32[]{:S(2)}) copy-start(bf16[512,512]{1,0:T(8,128)(2,1)} %copy-done.2) | copy-start | bytes 1572868
  121.6 133.0 %all-to-all-start.3 = ((bf16[128,32,1024]{2,1,0:T(8,128)(2,1)}), bf16[128,32,1024]{2,1,0:T(8,128)(2,1)}, u32[]{:S(2)}, u32[]{:S(2)}) async-start(bf16[128,32,1024]{2,1,0:T(8,128)(2,1)} %stack.2), calls=%async_computation.3 | async-start | bytes 16777216 | tf_op jit(solution)/shard_map/all_to_all | solution.py:72
  150.6 104.0 %copy-start.4 = (bf16[512,512]{1,0:T(8,128)(2,1)S(1)}, bf16[512,512]{1,0:T(8,128)(2,1)}, u32[]{:S(2)}) copy-start(bf16[512,512]{1,0:T(8,128)(2,1)} %get-tuple-element.5) | copy-start | bytes 1572868
Sparse Core Ops, SparseCore 0:
  91.1 156.4 all-gather.2
